TPU v7x, 256 devices: a whole 4x4x8 slice. The times are simulated.
256 devices in a mesh: ctx: 32 (over x_hi, z, core), ch: 8 (over y, x_lo).
Axes of the slice: x: 4 (x_hi: 2, x_lo: 2; x = x_hi * 2 + x_lo), y: 4, z: 8, core: 2. Of those that a mesh axis runs over, the one named last changes fastest.
Arguments:
- saved_input: bfloat16 [32, 16, 98304], P(None, 'ch', 'ctx'), may hold values from -6 to 6
- out_grad: bfloat16 [32, 16, 98304], P(None, 'ch', 'ctx'), may hold values from -6 to 6
- block_offsets: int32 [16], replicated, may hold values from 1 to 743, as said below
- head_len: int32 [1], replicated, may hold values from 16 to 128
Outputs:
- grad_filter: float32 [32, 2176], P(None, 'ctx')
Inputs may be any that keep to these rules, and one draw needn't show every extreme that they name: `block_offsets`: 16 distinct values; the largest is 743.
All inputs are finite; a program needn't handle non-finite values.
Results may differ from a plain program's by a relative error of at most 0.0003.
Values may be sent and summed in bfloat16 or wider, within the bound.
No kernel may reach another device: no remote copies, remote signals or barrier semaphores. Data moves between devices by JAX's collectives and lax.ppermute only.
A program may use at most 64 MiB of HBM per device.

v0:
```python
import math

import jax
import jax.numpy as jnp
from jax import lax
from jax.sharding import PartitionSpec as P


def sent_together(arrays, axis, split_dim, concat_dim, along):
    ends, at = ([], 0)
    for a in arrays[:-1]:
        at += a.shape[along]
        ends.append(at)
    both = jnp.concatenate(arrays, axis=along)
    return tuple(
        jnp.split(
            lax.all_to_all(both, axis, split_axis=split_dim, concat_axis=concat_dim, tiled=True),
            ends,
            axis=along,
        )
    )


def copy_for_each(shard, axis):
    size = lax.axis_size(axis)
    return lax.all_to_all(
        jnp.broadcast_to(shard[None], (size, *shard.shape)), axis, 0, 0, tiled=True
    )


def of_everyone(shard, axis):
    everything = copy_for_each(shard, axis)
    return jnp.sum(everything, axis=0)


def diagonals(lag_grid):
    filt_count = lag_grid.shape[0]
    diag_band = lag_grid.reshape(filt_count, -1)[:, 127 : 127 + 255 * 128].reshape(
        filt_count, 128, 255
    )[:, :, :128]
    return jnp.sum(diag_band, axis=1)


def tile_grad(dy_tiles, flipped_tiles, first_tile):
    filters, local_ch, tile_count, width = dy_tiles.shape
    left_tiles = lax.dynamic_slice_in_dim(flipped_tiles, first_tile, tile_count, 2)
    right_tiles = lax.dynamic_slice_in_dim(flipped_tiles, first_tile + 1, tile_count, 2)
    window = jnp.stack([right_tiles, left_tiles], axis=3)
    lag_grid = jnp.einsum("fgai,fgask->fisk", dy_tiles, window, preferred_element_type=jnp.float32)
    return diagonals(lag_grid.reshape(filters, 128, 256))


def head_masked(lag_terms, head_len):
    lag_index = lax.broadcasted_iota(jnp.int32, (1, lag_terms.shape[1]), 1)
    keep_mask = (lag_index >= 128) | (lag_index < head_len[0])
    return jnp.where(keep_mask, lag_terms, jnp.zeros_like(lag_terms))


def local(saved_input, out_grad, block_offsets, head_len):
    filters, local_ch, tok_dev = saved_input.shape
    tile_count = tok_dev // 128
    offsets = jnp.concatenate([jnp.zeros((1,), jnp.int32), block_offsets])
    block_count = offsets.shape[0]
    ctx_count = lax.axis_size("ctx")
    loss_scale = 1.0 / math.sqrt(tok_dev * ctx_count * local_ch * lax.axis_size("ch"))
    input_tiles = saved_input.reshape(filters, local_ch, tile_count, 128)[:, :, :, ::-1]
    grad_tiles = out_grad.reshape(filters, local_ch, tile_count, 128)
    own_input, own_grad = sent_together((input_tiles, grad_tiles), "ctx", 0, 2, 1)
    own_filters = own_input.shape[0]
    pad_tiles = (ctx_count - 1) * tile_count + 1
    padded_x = jnp.concatenate(
        [jnp.zeros((own_filters, local_ch, pad_tiles, 128), own_input.dtype), own_input], axis=2
    )

    def per_block(offset):
        return tile_grad(own_grad, padded_x, pad_tiles - offset - 1)

    own_sums = lax.map(per_block, offsets)
    own_terms = jnp.transpose(own_sums, (1, 0, 2)).reshape(own_filters, block_count * 128)
    own_terms = head_masked(own_terms, head_len)
    group_terms = of_everyone(own_terms, "ch")
    lag_piece = lax.all_to_all(group_terms, "ctx", split_axis=1, concat_axis=0, tiled=True)
    return lag_piece * loss_scale


def solution(mesh):
    in_specs = (P(None, "ch", "ctx"), P(None, "ch", "ctx"), P(), P())
    out_specs = P(None, "ctx")
    return jax.shard_map(local, mesh=mesh, in_specs=in_specs, out_specs=out_specs, check_vma=False)
```

profile of v0, /device:TPU:1, one launch (start us, length us, event | category | flops | bytes accessed | tf_op | source)
XLA Modules:
  0.0 153.7 jit_solution(14745305595088274148)
XLA Ops:
  0.0 1.2 reshape.86
  1.6 0.6 copy-done
  2.5 0.9 pad_maximum_fusion
  3.4 12.6 %all-to-all-start = ((bf16[32,4,24,128]{3,2,1,0:T(8,128)(2,1)}), bf16[32,4,24,128]{3,2,1,0:T(8,128)(2,1)S(1)}, u32[]{:S(2)}, u32[]{:S(2)}) async-start(bf16[32,4,24,128]{3,2,1,0:T(8,128)(2,1)} %pad_maximum_fusion), calls=%async_computation | async-start | bytes 1572864 | tf_op jit(solution)/shard_map/all_to_all | solution.py:17
  16.8 22.0 %all-to-all-done = bf16[32,4,24,128]{3,2,1,0:T(8,128)(2,1)S(1)} async-done(((bf16[32,4,24,128]{3,2,1,0:T(8,128)(2,1)}), bf16[32,4,24,128]{3,2,1,0:T(8,128)(2,1)S(1)}, u32[]{:S(2)}, u32[]{:S(2)}) %all-to-all-start) | async-done | bytes 786464 | tf_op jit(solution)/shard_map/all_to_all | solution.py:17
  39.3 87.6 %while.14 = (s32[]{:T(128)}, f32[17,1,128]{2,1,0:T(1,128)S(1)}, s32[17]{0:T(128)S(1)}, bf16[1,2,1513,128]{2,3,1,0:T(8,128)(2,1)S(1)}, bf16[1,2,768,128]{3,2,1,0:...) while((s32[]{:T(128)}, f32[17,1,128]{2,1,0:T(1,128)S(1)}, ...), condition=%wide.region_2.3_spmd, body=%wide.region_0.2_spmd.sunk | while | flops 101072776 | bytes 3735265 | solution.py:78
  39.4 0.7 dynamic_slice.33
  42.8 0.5 dynamic-slice_bitcast_fusion.3
  44.5 0.7 dynamic_slice.33
  49.7 0.7 dynamic_slice.33
  53.1 0.5 dynamic-slice_bitcast_fusion.3
  54.8 0.7 dynamic_slice.33
  60.0 0.7 dynamic_slice.33
  65.1 0.7 dynamic_slice.33
  70.3 0.7 dynamic_slice.33
  75.4 0.7 dynamic_slice.33
  80.6 0.7 dynamic_slice.33
  84.0 0.5 dynamic-slice_bitcast_fusion.3
  85.7 0.7 dynamic_slice.33
  90.9 0.7 dynamic_slice.33
  94.3 0.5 dynamic-slice_bitcast_fusion.3
  96.0 0.7 dynamic_slice.33
  101.2 0.7 dynamic_slice.33
  104.6 0.5 dynamic-slice_bitcast_fusion.3
  106.3 0.7 dynamic_slice.33
  111.5 0.7 dynamic_slice.33
  116.6 0.7 dynamic_slice.33
  121.8 0.7 dynamic_slice.33
  125.2 0.5 dynamic-slice_bitcast_fusion.3
  127.0 9.2 %all_to_all.36 = f32[8,1,2176]{2,1,0:T(1,128)S(1)} all-to-all(f32[8,1,2176]{2,1,0:T(1,128)S(1)} %broadcast_in_dim.25), channel_id=1, replica_groups=mesh['ctx'=32,'ch'=8] {'ch'}, dimensions={0} | all-to-all | bytes 139264 | tf_op jit(solution)/shard_map/all_to_all | solution.py:26
  136.4 16.7 %all_to_all.37 = f32[1,32,68]{2,0,1:T(1,128)S(1)} all-to-all(f32[1,32,68]{2,0,1:T(1,128)S(1)} %all_to_all.31), channel_id=1, replica_groups=mesh['ctx'=32,'ch'=8] {'ctx'}, dimensions={1} | all-to-all | bytes 17408 | tf_op jit(solution)/shard_map/all_to_all | solution.py:82
  153.1 0.6 broadcast_multiply_fusion
  (129 shorter events, 27.1 us)
Async XLA Ops:
  1.2 1.0 copy-start
  3.4 35.4 %all-to-all-start = ((bf16[32,4,24,128]{3,2,1,0:T(8,128)(2,1)}), bf16[32,4,24,128]{3,2,1,0:T(8,128)(2,1)S(1)}, u32[]{:S(2)}, u32[]{:S(2)}) async-start(bf16[32,4,24,128]{3,2,1,0:T(8,128)(2,1)} %pad_maximum_fusion), calls=%async_computation | async-start | bytes 1572864 | tf_op jit(solution)/shard_map/all_to_all | solution.py:17
  16.0 0.7 copy-start.1
where the time goes:
time: 155 us; the launch traced here: 154 us
  loops' own time  47.8 us (31%)
  local copies, waits for them, and re-layouts  36.3 us (23%)
  blocking collectives  25.9 us (17%)
  waiting for transfers between devices  22 us (14%)
  starting transfers between devices  12.6 us (8%)
  matrix products  6.01 us (4%)
  other arithmetic  2.3 us (1%)
    another operation x1, loops' own time, local(): own_sums = lax.map(per_block, offsets)  47.8 us
    all_to_all x1, waiting for transfers between devices, sent_together(): lax.all_to_all(both, axis, split_axis=split_dim, concat_axis=concat_dim,...  22 us
    all_to_all x1, blocking collectives, local(): lax.all_to_all(group_terms, 'ctx', split_axis=1, concat_axis=0, tiled=True)  16.7 us
    all_to_all x1, starting transfers between devices, sent_together(): lax.all_to_all(both, axis, split_axis=split_dim, concat_axis=concat_dim,...  12.6 us
    dynamic_slice x17, local copies, waits for them, and re-layouts, local(): own_sums = lax.map(per_block, offsets)  11.3 us
    all_to_all x1, blocking collectives, copy_for_each(): lax.all_to_all(jnp.broadcast_to(shard[None], (size, *shard.shape)), axis,...  9.22 us
    another operation x17, local copies, waits for them, and re-layouts, tile_grad(): window = jnp.stack([right_tiles, left_tiles], axis=3)  7.87 us
    slice x17, local copies, waits for them, and re-layouts, diagonals(): lag_grid.reshape(filt_count, -1)[:, 127:127 + 255 * 128]  6.22 us
  transfers between devices with their start and end apart: 1, of which 1 were waited for; matrix products, arithmetic and copies ran while one was open for 0% of the time, Pallas kernels for 0%

commit v1 on v0

v1 whole, which is shorter than its diff:
```python
import math

import jax
import jax.numpy as jnp
from jax import lax
from jax.experimental import pallas as pl
from jax.experimental.pallas import tpu as pltpu
from jax.sharding import PartitionSpec as P

LANES = 128


def lag_kernel(scale, offsets_ref, head_ref, both_ref, out_ref, x_ref, y_ref, xt_ref, diag_ref, sems):
    shards, pair_tiles = both_ref.shape[:2]
    per = pair_tiles // 2
    tiles = shards * per
    rows = 2 * tiles
    def shard_view(ref, first):
        return ref.at[pl.ds(first, tiles)].reshape(shards, per, 2, LANES)

    copies = [
        pltpu.make_async_copy(both_ref.at[:, pl.ds(0, per)], shard_view(x_ref, 1), sems.at[0]),
        pltpu.make_async_copy(both_ref.at[:, pl.ds(per, per)], shard_view(y_ref, 0), sems.at[1]),
    ]
    for c in copies:
        c.start()
    x_ref[0] = jnp.zeros((2, LANES), x_ref.dtype)
    y_tail = y_ref.at[pl.ds(tiles, tiles)].reshape(rows, LANES)
    y_tail[...] = jnp.zeros((rows, LANES), y_ref.dtype)
    for c in copies:
        c.wait()
    for part, first in ((0, 1), (1, 0)):
        xs = x_ref.at[pl.ds(first, tiles)].reshape(rows, LANES)
        xt_ref[pl.ds(part * LANES, LANES), :] = xs[...].T
    blocks = out_ref.shape[0]
    keep = lax.broadcasted_iota(jnp.int32, (LANES, LANES), 0) <= lax.broadcasted_iota(
        jnp.int32, (LANES, LANES), 1)
    xt = xt_ref[...]
    for k in range(0, blocks, 2):
        group = [j for j in (k, k + 1) if j < blocks]
        windows = []
        for j in group:
            start = 0 if j == 0 else offsets_ref[j - 1]
            windows.append(y_ref.at[pl.ds(start, tiles)].reshape(rows, LANES)[...])
        window = jnp.concatenate(windows, axis=1) if len(windows) > 1 else windows[0]
        grid = jnp.dot(xt, window, preferred_element_type=jnp.float32)
        for n, j in enumerate(group):
            part = grid[:, n * LANES:(n + 1) * LANES]
            both = jnp.where(keep, part[:LANES], part[LANES:])
            acc = both[:8]
            for v in range(1, LANES // 8):
                acc = acc + pltpu.roll(both[8 * v:8 * v + 8], LANES - 8 * v, 1)
            diag_ref[pl.ds(8 * j, 8), :] = acc
    acc = diag_ref[...]
    sub = lax.broadcasted_iota(jnp.int32, acc.shape, 0)
    for bit in (1, 2, 4):
        acc = jnp.where((sub & bit) != 0, pltpu.roll(acc, LANES - bit, 1), acc)
    sums = jnp.sum(acc.reshape(blocks, 8, LANES), axis=1) * scale
    block = lax.broadcasted_iota(jnp.int32, sums.shape, 0)
    lag = lax.broadcasted_iota(jnp.int32, sums.shape, 1)
    out_ref[...] = jnp.where((block > 0) | (lag < head_ref[0]), sums, jnp.zeros_like(sums))


def lag_sums(both, offsets, head_len, scale):
    shards, pair_tiles = both.shape[:2]
    tiles = shards * pair_tiles // 2
    blocks = offsets.shape[0] + 1
    return pl.pallas_call(
        lambda *refs: lag_kernel(scale, *refs),
        out_shape=jax.ShapeDtypeStruct((blocks, LANES), jnp.float32),
        in_specs=[
            pl.BlockSpec(memory_space=pltpu.SMEM),
            pl.BlockSpec(memory_space=pltpu.SMEM),
            pl.BlockSpec(memory_space=pl.ANY),
        ],
        out_specs=pl.BlockSpec(memory_space=pltpu.VMEM),
        scratch_shapes=[
            pltpu.VMEM((tiles + 1, 2, LANES), both.dtype),
            pltpu.VMEM((2 * tiles, 2, LANES), both.dtype),
            pltpu.VMEM((2 * LANES, 2 * tiles), both.dtype),
            pltpu.VMEM((8 * blocks, LANES), jnp.float32),
            pltpu.SemaphoreType.DMA((2,)),
        ],
    )(offsets, head_len, both)


def local(saved_input, out_grad, block_offsets, head_len):
    filters, local_ch, tok_dev = saved_input.shape
    ctx_count, ch_count = lax.axis_size("ctx"), lax.axis_size("ch")
    scale = 1.0 / math.sqrt(tok_dev * ctx_count * local_ch * ch_count)
    both = jnp.concatenate([saved_input, out_grad], axis=2)
    both = lax.all_to_all(both, "ctx", split_axis=0, concat_axis=0, tiled=True)
    tiles = both.shape[2] // LANES
    both = both.reshape(ctx_count, local_ch, tiles, LANES).transpose(0, 2, 1, 3)
    sums = lag_sums(both, block_offsets, head_len, scale)
    pieces = sums.reshape(ctx_count, 1, -1)
    pieces = jnp.broadcast_to(pieces, (ctx_count, ch_count, pieces.shape[2]))
    pieces = pieces.reshape(ctx_count * ch_count, -1)
    got = lax.all_to_all(pieces, ("ctx", "ch"), split_axis=0, concat_axis=0, tiled=True)
    return jnp.sum(got.reshape(filters, ch_count, -1), axis=1)


def solution(mesh):
    in_specs = (P(None, "ch", "ctx"), P(None, "ch", "ctx"), P(), P())
    return jax.shard_map(
        local, mesh=mesh, in_specs=in_specs, out_specs=P(None, "ctx"), check_vma=False
    )
```

time: 155 us -> 68.7 us (0.44)
  loops' own time: 47.8 us -> 0 us
  local copies, waits for them, and re-layouts: 36.3 us -> 1.7 us
  Pallas kernels: 0 us -> 6.73 us
  matrix products: 6.01 us -> 0 us
  blocking collectives: 25.9 us -> 21.2 us
    another operation x1 -> x0, loops' own time: 47.8 us -> none  [local(): own_sums = lax.map(per_block, offsets)]
    dynamic_slice x17 -> x0, local copies, waits for them, and re-layouts: 11.3 us -> none  [local(): own_sums = lax.map(per_block, offsets)]
    another operation x17 -> x0, local copies, waits for them, and re-layouts: 7.87 us -> none  [tile_grad(): window = jnp.stack([right_tiles, left_tiles], axis=3)]
    reshape x19 -> x0, local copies, waits for them, and re-layouts: 7.17 us -> none  [the longest x17 5.67 us: diagonals(): lag_grid.reshape(filt_count, -1)[:, 127:127 + 255 * 128]]
    pallas_call x0 -> x1, Pallas kernels: none -> 6.73 us  [lag_sums(): pl.pallas_call(lambda *refs: lag_kernel(scale, *refs), out_shape=jax.Shap...]
    slice x17 -> x0, local copies, waits for them, and re-layouts: 6.22 us -> none  [diagonals(): lag_grid.reshape(filt_count, -1)[:, 127:127 + 255 * 128]]
    dot_general x17 -> x0, matrix products: 6.01 us -> none  [tile_grad(): jnp.einsum('fgai,fgask->fisk', dy_tiles, window, preferred_element_type=j...]
    all_to_all x2 -> x1, blocking collectives: 25.9 us -> 21.2 us  [local(): lax.all_to_all(pieces, ('ctx', 'ch'), split_axis=0, concat_axis=0, tiled=...]
where the time goes in v1:
time: 68.7 us; the launch traced here: 68.4 us
  waiting for transfers between devices  22.1 us (32%)
  blocking collectives  21.2 us (31%)
  starting transfers between devices  12.6 us (18%)
  Pallas kernels  6.73 us (10%)
  other arithmetic  3.35 us (5%)
  local copies, waits for them, and re-layouts  1.7 us (2%)
    all_to_all x1, waiting for transfers between devices, local(): both = lax.all_to_all(both, 'ctx', split_axis=0, concat_axis=0, tiled=True)  22.1 us
    all_to_all x1, blocking collectives, local(): lax.all_to_all(pieces, ('ctx', 'ch'), split_axis=0, concat_axis=0, tiled=...  21.2 us
    all_to_all x1, starting transfers between devices, local(): both = lax.all_to_all(both, 'ctx', split_axis=0, concat_axis=0, tiled=True)  12.6 us
    pallas_call x1, Pallas kernels, lag_sums(): pl.pallas_call(lambda *refs: lag_kernel(scale, *refs), out_shape=jax.Shap...  6.73 us
    concatenate x1, other arithmetic, local(): both = jnp.concatenate([saved_input, out_grad], axis=2)  2.71 us
  transfers between devices with their start and end apart: 1, of which 1 were waited for; matrix products, arithmetic and copies ran while one was open for 0% of the time, Pallas kernels for 0%

profile of v1, /device:TPU:1, one launch (start us, length us, event | category | flops | bytes accessed | tf_op | source)
XLA Modules:
  0.0 68.4 jit_solution(10004329701132273544)
XLA Ops:
  0.0 2.7 %pad_maximum_fusion = bf16[32,2,6144]{2,1,0:T(2,128)(2,1)} fusion(bf16[32,2,3072]{2,1,0:T(2,128)(2,1)} %param.5, bf16[32,2,3072]{2,1,0:T(2,128)(2,1)} %param.4), kind=kLoop, calls=%fused_computation | loop fusion | flops 1572864 | bytes 1572864 | tf_op jit(solution)/shard_map/concatenate | solution.py:91
  2.7 12.6 %all-to-all-start = ((bf16[32,2,6144]{2,1,0:T(2,128)(2,1)}), bf16[32,2,6144]{2,1,0:T(2,128)(2,1)S(1)}, u32[]{:S(2)}, u32[]{:S(2)}) async-start(bf16[32,2,6144]{2,1,0:T(2,128)(2,1)} %pad_maximum_fusion), calls=%async_computation | async-start | bytes 1572864 | tf_op jit(solution)/shard_map/all_to_all | solution.py:92
  15.9 22.1 %all-to-all-done = bf16[32,2,6144]{2,1,0:T(2,128)(2,1)S(1)} async-done(((bf16[32,2,6144]{2,1,0:T(2,128)(2,1)}), bf16[32,2,6144]{2,1,0:T(2,128)(2,1)S(1)}, u32[]{:S(2)}, u32[]{:S(2)}) %all-to-all-start) | async-done | bytes 786464 | tf_op jit(solution)/shard_map/all_to_all | solution.py:92
  38.1 0.0 copy-start
  38.1 0.9 %copy-done = bf16[32,2,6144]{2,1,0:T(2,128)(2,1)} copy-done((bf16[32,2,6144]{2,1,0:T(2,128)(2,1)}, bf16[32,2,6144]{2,1,0:T(2,128)(2,1)S(1)}, u32[]{:S(2)}) %copy-start) | copy-done | bytes 786456
  39.0 6.7 %shard_map.46 = f32[17,128]{1,0:T(8,128)} custom-call(s32[16]{0:T(128)} %refs_0_.1, s32[1]{0:T(128)S(6)} %copy.5.refs_1_, bf16[32,48,2,128]{3,2,1,0:T(2,128)(2,1)} %bitcast.7), custom_call_target="tpu_custom_call" | custom-call | tf_op jit(solution)/shard_map/pallas_call | solution.py:68
  45.7 0.8 %broadcast_in_dim.7 = f32[32,68]{1,0:T(8,128)S(1)} reshape(f32[17,128]{1,0:T(8,128)} %shard_map.46) | data formatting | bytes 17408 | tf_op jit(solution)/shard_map/broadcast_in_dim | solution.py:97
  46.5 21.2 %all_to_all.14 = f32[256,1,68]{2,1,0:T(1,128)S(1)} all-to-all(f32[256,1,68]{2,1,0:T(1,128)S(1)} %bitcast.8), channel_id=1, replica_groups=mesh['ctx'=32,'ch'=8] {'ctx','ch'}, dimensions={0} | all-to-all | bytes 139264 | tf_op jit(solution)/shard_map/all_to_all | solution.py:99
  67.8 0.6 bitcast_reduce_fusion
  (1 shorter events, 0.0 us)
Async XLA Ops:
  2.7 35.4 %all-to-all-start = ((bf16[32,2,6144]{2,1,0:T(2,128)(2,1)}), bf16[32,2,6144]{2,1,0:T(2,128)(2,1)S(1)}, u32[]{:S(2)}, u32[]{:S(2)}) async-start(bf16[32,2,6144]{2,1,0:T(2,128)(2,1)} %pad_maximum_fusion), calls=%async_computation | async-start | bytes 1572864 | tf_op jit(solution)/shard_map/all_to_all | solution.py:92
  38.1 0.9 %copy-start = (bf16[32,2,6144]{2,1,0:T(2,128)(2,1)}, bf16[32,2,6144]{2,1,0:T(2,128)(2,1)S(1)}, u32[]{:S(2)}) copy-start(bf16[32,2,6144]{2,1,0:T(2,128)(2,1)S(1)} %all-to-all-done) | copy-start | bytes 2359300

commit v2 on v1

v2 whole, which is shorter than its diff:
```python
import functools
import math

import jax
import jax.numpy as jnp
from jax import lax
from jax.experimental import pallas as pl
from jax.experimental.pallas import tpu as pltpu
from jax.sharding import PartitionSpec as P

LANES = 128
VMEM = pl.BlockSpec(memory_space=pltpu.VMEM)
SMEM = pl.BlockSpec(memory_space=pltpu.SMEM)
ANY = pl.BlockSpec(memory_space=pl.ANY)


def join_kernel(a_ref, b_ref, out_ref, sems):
    width = a_ref.shape[2]
    copies = [
        pltpu.make_async_copy(a_ref, out_ref.at[:, :, pl.ds(0, width)], sems.at[0]),
        pltpu.make_async_copy(b_ref, out_ref.at[:, :, pl.ds(width, width)], sems.at[1]),
    ]
    for c in copies:
        c.start()
    for c in copies:
        c.wait()


def joined(a, b):
    return pl.pallas_call(
        join_kernel,
        out_shape=pltpu.VMEM((*a.shape[:2], 2 * a.shape[2]), a.dtype),
        in_specs=[ANY, ANY],
        out_specs=VMEM,
        scratch_shapes=[pltpu.SemaphoreType.DMA((2,))],
    )(a, b)


def lag_kernel(scale, offsets_ref, head_ref, both_ref, out_ref, x_ref, y_ref, xt_ref, diag_ref):
    shards, pair_tiles = both_ref.shape[:2]
    per = pair_tiles // 2
    tiles = shards * per
    rows = 2 * tiles

    def flat(ref, first, count):
        return ref.at[pl.ds(first, count)].reshape(2 * count, LANES)

    x_ref[0] = jnp.zeros((2, LANES), x_ref.dtype)
    flat(y_ref, tiles, tiles)[...] = jnp.zeros((rows, LANES), y_ref.dtype)

    def split(s, carry):
        flat(x_ref, 1 + s * per, per)[...] = flat(both_ref.at[s], 0, per)[...]
        flat(y_ref, s * per, per)[...] = flat(both_ref.at[s], per, per)[...]
        return carry

    lax.fori_loop(0, shards, split, 0, unroll=8)
    for part, first in ((0, 1), (1, 0)):
        xt_ref[pl.ds(part * LANES, LANES), :] = flat(x_ref, first, tiles)[...].T
    blocks = diag_ref.shape[0] // 8
    keep = lax.broadcasted_iota(jnp.int32, (LANES, LANES), 0) <= lax.broadcasted_iota(
        jnp.int32, (LANES, LANES), 1)
    xt = xt_ref[...]
    for k in range(0, blocks, 2):
        group = [j for j in (k, k + 1) if j < blocks]
        windows = [
            flat(y_ref, 0 if j == 0 else offsets_ref[j - 1], tiles)[...] for j in group
        ]
        window = jnp.concatenate(windows, axis=1) if len(windows) > 1 else windows[0]
        grid = jnp.dot(xt, window, preferred_element_type=jnp.float32)
        for n, j in enumerate(group):
            part = grid[:, n * LANES:(n + 1) * LANES]
            both = jnp.where(keep, part[:LANES], part[LANES:])
            acc = both[:8]
            for v in range(1, LANES // 8):
                acc = acc + pltpu.roll(both[8 * v:8 * v + 8], LANES - 8 * v, 1)
            diag_ref[pl.ds(8 * j, 8), :] = acc
    acc = diag_ref[...]
    sub = lax.broadcasted_iota(jnp.int32, acc.shape, 0)
    for bit in (1, 2, 4):
        acc = jnp.where((sub & bit) != 0, pltpu.roll(acc, LANES - bit, 1), acc)
    sums = jnp.sum(acc.reshape(blocks, 8, LANES), axis=1) * scale
    block = lax.broadcasted_iota(jnp.int32, sums.shape, 0)
    lag = lax.broadcasted_iota(jnp.int32, sums.shape, 1)
    sums = jnp.where((block > 0) | (lag < head_ref[0]), sums, jnp.zeros_like(sums))
    pieces, copies, width = out_ref.shape
    lane = lax.broadcasted_iota(jnp.int32, (copies, LANES), 1)
    for q in range(pieces):
        b, s = divmod(q * width, LANES)
        row = jnp.broadcast_to(sums[b:b + 1], (copies, LANES))
        if s:
            row = pltpu.roll(row, LANES - s, 1)
        if s + width > LANES:
            after = jnp.broadcast_to(sums[b + 1:b + 2], (copies, LANES))
            row = jnp.where(lane < LANES - s, row, pltpu.roll(after, LANES - s, 1))
        out_ref[q] = row[:, :width]


def lag_sums(both, offsets, head_len, scale, pieces, copies):
    shards, pair_tiles = both.shape[:2]
    tiles = shards * pair_tiles // 2
    blocks = offsets.shape[0] + 1
    return pl.pallas_call(
        functools.partial(lag_kernel, scale),
        out_shape=pltpu.VMEM((pieces, copies, blocks * LANES // pieces), jnp.float32),
        in_specs=[SMEM, SMEM, VMEM],
        out_specs=VMEM,
        scratch_shapes=[
            pltpu.VMEM((tiles + 1, 2, LANES), both.dtype),
            pltpu.VMEM((2 * tiles, 2, LANES), both.dtype),
            pltpu.VMEM((2 * LANES, 2 * tiles), both.dtype),
            pltpu.VMEM((8 * blocks, LANES), jnp.float32),
        ],
    )(offsets, head_len, pltpu.with_memory_space_constraint(both, pltpu.VMEM))


def local(saved_input, out_grad, block_offsets, head_len):
    filters, local_ch, tok_dev = saved_input.shape
    ctx_count, ch_count = lax.axis_size("ctx"), lax.axis_size("ch")
    scale = 1.0 / math.sqrt(tok_dev * ctx_count * local_ch * ch_count)
    both = joined(saved_input, out_grad)
    both = lax.all_to_all(both, "ctx", split_axis=0, concat_axis=0, tiled=True)
    tiles = both.shape[2] // LANES
    both = both.reshape(ctx_count, local_ch, tiles, LANES).transpose(0, 2, 1, 3)
    sums = lag_sums(both, block_offsets, head_len, scale, ctx_count, ch_count)
    sums = sums.reshape(ctx_count * ch_count, -1)
    got = lax.all_to_all(sums, ("ctx", "ch"), split_axis=0, concat_axis=0, tiled=True)
    return jnp.sum(got.reshape(filters, ch_count, -1), axis=1)


def solution(mesh):
    in_specs = (P(None, "ch", "ctx"), P(None, "ch", "ctx"), P(), P())
    return jax.shard_map(
        local, mesh=mesh, in_specs=in_specs, out_specs=P(None, "ctx"), check_vma=False
    )
```

time: 68.7 us -> 64.9 us (0.945)
  other arithmetic: 3.35 us -> 0.64 us
  local copies, waits for them, and re-layouts: 1.7 us -> 0 us
    concatenate x1 -> x0, other arithmetic: 2.71 us -> none  [local(): both = jnp.concatenate([saved_input, out_grad], axis=2)]
    unnamed x2 -> x0, local copies, waits for them, and re-layouts: 0.88 us -> none
    broadcast_in_dim x2 -> x0, local copies, waits for them, and re-layouts: 0.82 us -> none  [local(): pieces = jnp.broadcast_to(pieces, (ctx_count, ch_count, pieces.shape[2]))]
    pallas_call x1 -> x2, Pallas kernels: 6.73 us -> 7.37 us  [the longest x1 5.36 us: lag_sums(): pl.pallas_call(functools.partial(lag_kernel, scale), out_shape=pltpu.VMEM...]
where the time goes in v2:
time: 64.9 us; the launch traced here: 64.6 us
  waiting for transfers between devices  22.1 us (34%)
  blocking collectives  21.2 us (33%)
  starting transfers between devices  12.6 us (19%)
  Pallas kernels  7.37 us (11%)
  between operations  0.67 us (1%)
    all_to_all x1, waiting for transfers between devices, local(): both = lax.all_to_all(both, 'ctx', split_axis=0, concat_axis=0, tiled=True)  22.1 us
    all_to_all x1, blocking collectives, local(): lax.all_to_all(sums, ('ctx', 'ch'), split_axis=0, concat_axis=0, tiled=True)  21.2 us
    all_to_all x1, starting transfers between devices, local(): both = lax.all_to_all(both, 'ctx', split_axis=0, concat_axis=0, tiled=True)  12.6 us
    pallas_call x1, Pallas kernels, lag_sums(): pl.pallas_call(functools.partial(lag_kernel, scale), out_shape=pltpu.VMEM...  5.36 us
    pallas_call x1, Pallas kernels, joined(): pl.pallas_call(join_kernel, out_shape=pltpu.VMEM((*a.shape[:2], 2 * a.sha...  2.01 us
  transfers between devices with their start and end apart: 1, of which 1 were waited for; matrix products, arithmetic and copies ran while one was open for 0% of the time, Pallas kernels for 0%

profile of v2, /device:TPU:1, one launch (start us, length us, event | category | flops | bytes accessed | tf_op | source)
XLA Modules:
  0.0 64.6 jit_solution(2416084140206194717)
XLA Ops:
  0.0 2.0 %shard_map.46 = bf16[32,2,6144]{2,1,0:T(2,128)(2,1)} custom-call(bf16[32,2,3072]{2,1,0:T(2,128)(2,1)} %a_ref.1, bf16[32,2,3072]{2,1,0:T(2,128)(2,1)} %b_ref.1), custom_call_target="tpu_custom_call" | custom-call | tf_op jit(solution)/shard_map/pallas_call | solution.py:30
  2.0 12.6 %all-to-all-start = ((bf16[32,2,6144]{2,1,0:T(2,128)(2,1)}), bf16[32,2,6144]{2,1,0:T(2,128)(2,1)S(1)}, u32[]{:S(2)}, u32[]{:S(2)}) async-start(bf16[32,2,6144]{2,1,0:T(2,128)(2,1)} %shard_map.46), calls=%async_computation | async-start | bytes 1572864 | tf_op jit(solution)/shard_map/all_to_all | solution.py:121
  15.3 22.1 %all-to-all-done = bf16[32,2,6144]{2,1,0:T(2,128)(2,1)S(1)} async-done(((bf16[32,2,6144]{2,1,0:T(2,128)(2,1)}), bf16[32,2,6144]{2,1,0:T(2,128)(2,1)S(1)}, u32[]{:S(2)}, u32[]{:S(2)}) %all-to-all-start) | async-done | bytes 786464 | tf_op jit(solution)/shard_map/all_to_all | solution.py:121
  37.4 5.4 %shard_map.47 = f32[32,8,68]{2,1,0:T(8,128)S(1)} custom-call(s32[16]{0:T(128)} %offsets_ref.1, s32[1]{0:T(128)S(6)} %copy.6.head_ref, bf16[32,48,2,128]{3,2,1,0:T(2,128)(2,1)S(1)} %bitcast.9), custom_call_target="tpu_custom_call" | custom-call | tf_op jit(solution)/shard_map/pallas_call | solution.py:102
  42.8 21.2 %all_to_all.14 = f32[256,1,68]{2,1,0:T(1,128)S(1)} all-to-all(f32[256,1,68]{2,1,0:T(1,128)S(1)} %bitcast.10), channel_id=1, replica_groups=mesh['ctx'=32,'ch'=8] {'ctx','ch'}, dimensions={0} | all-to-all | bytes 139264 | tf_op jit(solution)/shard_map/all_to_all | solution.py:126
  64.0 0.6 bitcast_reduce_fusion
Async XLA Ops:
  2.0 35.4 %all-to-all-start = ((bf16[32,2,6144]{2,1,0:T(2,128)(2,1)}), bf16[32,2,6144]{2,1,0:T(2,128)(2,1)S(1)}, u32[]{:S(2)}, u32[]{:S(2)}) async-start(bf16[32,2,6144]{2,1,0:T(2,128)(2,1)} %shard_map.46), calls=%async_computation | async-start | bytes 1572864 | tf_op jit(solution)/shard_map/all_to_all | solution.py:121

commit v3 on v2

v3 whole, which is shorter than its diff:
```python
import functools
import math

import jax
import jax.numpy as jnp
from jax import lax
from jax.experimental import pallas as pl
from jax.experimental.pallas import tpu as pltpu
from jax.sharding import PartitionSpec as P

LANES = 128
VMEM = pl.BlockSpec(memory_space=pltpu.VMEM)
ANY = pl.BlockSpec(memory_space=pl.ANY)


def join_kernel(offsets_hbm, a_ref, b_ref, out_ref, order_ref, offsets_ref, sems):
    width = a_ref.shape[2]
    fetch = pltpu.make_async_copy(offsets_hbm, offsets_ref, sems.at[2])
    fetch.start()
    copies = [
        pltpu.make_async_copy(a_ref, out_ref.at[:, :, pl.ds(0, width)], sems.at[0]),
        pltpu.make_async_copy(b_ref, out_ref.at[:, :, pl.ds(width, width)], sems.at[1]),
    ]
    for c in copies:
        c.start()
    fetch.wait()
    blocks = offsets_ref.shape[0] + 1
    shape = (-(-blocks // 8) * 8, LANES)
    sub = lax.broadcasted_iota(jnp.int32, shape, 0)
    lane = lax.broadcasted_iota(jnp.int32, shape, 1)
    down = across = jnp.zeros(shape, jnp.int32)
    for k in range(1, blocks):
        down = jnp.where(sub == k, offsets_ref[k - 1], down)
        across = jnp.where(lane == k, offsets_ref[k - 1], across)
    below = (across < down) & (lane < blocks)
    rank = jnp.sum(below.astype(jnp.int32), axis=1, keepdims=True)
    here = (rank == lane) & (sub < blocks)
    order_ref[0:1] = jnp.sum(jnp.where(here, down, 0), axis=0, keepdims=True)
    order_ref[1:2] = jnp.sum(jnp.where(here, sub, 0), axis=0, keepdims=True)
    for c in copies:
        c.wait()


def joined(offsets, a, b):
    return pl.pallas_call(
        join_kernel,
        out_shape=(
            pltpu.VMEM((*a.shape[:2], 2 * a.shape[2]), a.dtype),
            pltpu.VMEM((8, LANES), jnp.int32),
        ),
        in_specs=[ANY, ANY, ANY],
        out_specs=(VMEM, VMEM),
        scratch_shapes=[
            pltpu.SMEM(offsets.shape, offsets.dtype),
            pltpu.SemaphoreType.DMA((3,)),
        ],
    )(offsets, a, b)


def lag_kernel(scale, order_vmem, both_ref, out_ref, order_ref, x_ref, y_ref, xt_ref, diag_ref, sem):
    fetch = pltpu.make_async_copy(order_vmem, order_ref, sem)
    fetch.start()
    shards, pair_tiles = both_ref.shape[:2]
    per = pair_tiles // 2
    tiles = shards * per
    rows = 2 * tiles

    def flat(ref, first, count):
        return ref.at[pl.ds(first, count)].reshape(2 * count, LANES)

    x_ref[0] = jnp.zeros((2, LANES), x_ref.dtype)
    flat(y_ref, tiles, y_ref.shape[0] - tiles)[...] = jnp.zeros(
        (2 * (y_ref.shape[0] - tiles), LANES), y_ref.dtype)

    def split(s, carry):
        flat(x_ref, 1 + s * per, per)[...] = flat(both_ref.at[s], 0, per)[...]
        flat(y_ref, s * per, per)[...] = flat(both_ref.at[s], per, per)[...]
        return carry

    lax.fori_loop(0, shards, split, 0, unroll=8)
    for part, first in ((0, 1), (1, 0)):
        xt_ref[pl.ds(part * LANES, LANES), :] = flat(x_ref, first, tiles)[...].T
    fetch.wait()
    blocks = diag_ref.shape[0] // 8
    chunks = tiles // LANES
    keep = lax.broadcasted_iota(jnp.int32, (LANES, LANES), 0) <= lax.broadcasted_iota(
        jnp.int32, (LANES, LANES), 1)

    def work(places, count):
        windows = [flat(y_ref, order_ref[0, p], count * LANES)[...] for p in places]
        window = jnp.concatenate(windows, axis=1) if len(windows) > 1 else windows[0]
        grid = jnp.dot(xt_ref[:, :2 * count * LANES], window, preferred_element_type=jnp.float32)
        for n, p in enumerate(places):
            part = grid[:, n * LANES:(n + 1) * LANES]
            both = jnp.where(keep, part[:LANES], part[LANES:])
            acc = both[:8]
            for v in range(1, LANES // 8):
                acc = acc + pltpu.roll(both[8 * v:8 * v + 8], LANES - 8 * v, 1)
            diag_ref[pl.ds(pl.multiple_of(8 * order_ref[1, p], 8), 8), :] = acc

    half = blocks // 4 * 2
    for p in range(0, half, 2):
        work((p, p + 1), chunks)
    needed = (tiles - order_ref[0, half] + LANES - 1) // LANES
    for count in range(1, chunks + 1):
        @pl.when(needed == count)
        def _(count=count):
            for p in range(half, blocks, 2):
                work(tuple(range(p, min(p + 2, blocks))), count)

    acc = diag_ref[...]
    sub = lax.broadcasted_iota(jnp.int32, acc.shape, 0)
    for bit in (1, 2, 4):
        acc = jnp.where((sub & bit) != 0, pltpu.roll(acc, LANES - bit, 1), acc)
    sums = jnp.sum(acc.reshape(blocks, 8, LANES), axis=1) * scale
    pieces, copies, width = out_ref.shape
    lane = lax.broadcasted_iota(jnp.int32, (copies, LANES), 1)
    for q in range(pieces):
        b, s = divmod(q * width, LANES)
        row = jnp.broadcast_to(sums[b:b + 1], (copies, LANES))
        if s:
            row = pltpu.roll(row, LANES - s, 1)
        if s + width > LANES:
            after = jnp.broadcast_to(sums[b + 1:b + 2], (copies, LANES))
            row = jnp.where(lane < LANES - s, row, pltpu.roll(after, LANES - s, 1))
        out_ref[q] = row[:, :width]


def lag_sums(both, order, blocks, scale, pieces, copies):
    shards, pair_tiles = both.shape[:2]
    tiles = shards * pair_tiles // 2
    return pl.pallas_call(
        functools.partial(lag_kernel, scale),
        out_shape=jax.ShapeDtypeStruct((pieces, copies, blocks * LANES // pieces), jnp.float32),
        in_specs=[VMEM, VMEM],
        out_specs=VMEM,
        scratch_shapes=[
            pltpu.SMEM(order.shape, order.dtype),
            pltpu.VMEM((tiles + 1, 2, LANES), both.dtype),
            pltpu.VMEM((2 * tiles + LANES, 2, LANES), both.dtype),
            pltpu.VMEM((2 * LANES, 2 * tiles), both.dtype),
            pltpu.VMEM((8 * blocks, LANES), jnp.float32),
            pltpu.SemaphoreType.DMA,
        ],
    )(*(pltpu.with_memory_space_constraint(a, pltpu.VMEM) for a in (order, both)))


def local(saved_input, out_grad, block_offsets, head_len):
    filters, local_ch, tok_dev = saved_input.shape
    ctx_count, ch_count = lax.axis_size("ctx"), lax.axis_size("ch")
    scale = 1.0 / math.sqrt(tok_dev * ctx_count * local_ch * ch_count)
    both, order = joined(block_offsets, saved_input, out_grad)
    both = lax.all_to_all(both, "ctx", split_axis=0, concat_axis=0, tiled=True)
    tiles = both.shape[2] // LANES
    both = both.reshape(ctx_count, local_ch, tiles, LANES).transpose(0, 2, 1, 3)
    blocks = block_offsets.shape[0] + 1
    sums = lag_sums(both, order, blocks, scale, ctx_count, ch_count)
    sums = sums.reshape(ctx_count * ch_count, -1)
    got = lax.all_to_all(sums, ("ctx", "ch"), split_axis=0, concat_axis=0, tiled=True)
    out = jnp.sum(got.reshape(filters, ch_count, -1), axis=1)
    lag = lax.broadcasted_iota(jnp.int32, out.shape, 1) + lax.axis_index("ctx") * out.shape[1]
    return jnp.where((lag >= LANES) | (lag < head_len[0]), out, jnp.zeros_like(out))


def solution(mesh):
    in_specs = (P(None, "ch", "ctx"), P(None, "ch", "ctx"), P(), P())
    return jax.shard_map(
        local, mesh=mesh, in_specs=in_specs, out_specs=P(None, "ctx"), check_vma=False
    )
```

time: 64.9 us -> 63.8 us (0.983)
  blocking collectives: 21.2 us -> 35.2 us
  waiting for transfers between devices: 22.1 us -> 12.1 us
  starting transfers between devices: 12.6 us -> 8.65 us
  Pallas kernels: 7.37 us -> 6.29 us
    all_to_all x1, blocking collectives: 21.2 us -> 35.2 us  [local(): both = lax.all_to_all(both, 'ctx', split_axis=0, concat_axis=0, tiled=True)]
    all_to_all x1, waiting for transfers between devices: 22.1 us -> 12.1 us  [local(): lax.all_to_all(sums, ('ctx', 'ch'), split_axis=0, concat_axis=0, tiled=True)]
    all_to_all x1, starting transfers between devices: 12.6 us -> 8.65 us  [local(): lax.all_to_all(sums, ('ctx', 'ch'), split_axis=0, concat_axis=0, tiled=True)]
    pallas_call x2, Pallas kernels: 7.37 us -> 6.29 us  [the longest x1 5.15 us: lag_sums(): pl.pallas_call(functools.partial(lag_kernel, scale), out_shape=jax.ShapeD...]
where the time goes in v3:
time: 63.8 us; the launch traced here: 63.6 us
  blocking collectives  35.2 us (55%)
  waiting for transfers between devices  12.1 us (19%)
  starting transfers between devices  8.65 us (14%)
  Pallas kernels  6.29 us (10%)
  between operations  0.68 us (1%)
  other arithmetic  0.66 us (1%)
    all_to_all x1, blocking collectives, local(): both = lax.all_to_all(both, 'ctx', split_axis=0, concat_axis=0, tiled=True)  35.2 us
    all_to_all x1, waiting for transfers between devices, local(): lax.all_to_all(sums, ('ctx', 'ch'), split_axis=0, concat_axis=0, tiled=True)  12.1 us
    all_to_all x1, starting transfers between devices, local(): lax.all_to_all(sums, ('ctx', 'ch'), split_axis=0, concat_axis=0, tiled=True)  8.65 us
    pallas_call x1, Pallas kernels, lag_sums(): pl.pallas_call(functools.partial(lag_kernel, scale), out_shape=jax.ShapeD...  5.15 us
  transfers between devices with their start and end apart: 1, of which 1 were waited for; matrix products, arithmetic and copies ran while one was open for 0% of the time, Pallas kernels for 0%

profile of v3, /device:TPU:1, one launch (start us, length us, event | category | flops | bytes accessed | tf_op | source)
XLA Modules:
  0.0 63.6 jit_solution(8888737115939611428)
XLA Ops:
  0.0 1.1 %shard_map.46 = (bf16[32,2,6144]{2,1,0:T(2,128)(2,1)S(1)}, s32[8,128]{1,0:T(8,128)S(1)}) custom-call(s32[16]{0:T(128)} %offsets_hbm.1, bf16[32,2,3072]{2,1,0:T(2,128)(2,1)} %a_ref.1, bf16[32,2,3072]{2,1,0:T(2,128)(2,1)} %b_ref.1), custom_call_target="tpu_custom_call" | custom-call | tf_op jit(solution)/shard_map/pallas_call | solution.py:45
  1.1 35.2 %all_to_all.14 = bf16[32,2,6144]{2,1,0:T(2,128)(2,1)S(1)} all-to-all(bf16[32,2,6144]{2,1,0:T(2,128)(2,1)S(1)} %get-tuple-element.8), channel_id=1, replica_groups=mesh['ctx'=32,'ch'=8] {'ctx'}, dimensions={0} | all-to-all | bytes 1572864 | tf_op jit(solution)/shard_map/all_to_all | solution.py:153
  36.3 5.1 %shard_map.47 = f32[32,8,68]{2,1,0:T(8,128)} custom-call(s32[8,128]{1,0:T(8,128)S(1)} %get-tuple-element.7.order_vmem, bf16[32,48,2,128]{3,2,1,0:T(2,128)(2,1)S(1)} %bitcast.11), custom_call_target="tpu_custom_call" | custom-call | tf_op jit(solution)/shard_map/pallas_call | solution.py:132
  41.5 8.6 %all-to-all-start.1 = ((f32[256,1,68]{2,1,0:T(1,128)}), f32[256,1,68]{2,1,0:T(1,128)S(1)}, u32[]{:S(2)}, u32[]{:S(2)}) async-start(f32[256,1,68]{2,1,0:T(1,128)} %bitcast.12), calls=%async_computation.1 | async-start | bytes 262144 | tf_op jit(solution)/shard_map/all_to_all | solution.py:159
  50.8 12.1 %all-to-all-done.1 = f32[256,1,68]{2,1,0:T(1,128)S(1)} async-done(((f32[256,1,68]{2,1,0:T(1,128)}), f32[256,1,68]{2,1,0:T(1,128)S(1)}, u32[]{:S(2)}, u32[]{:S(2)}) %all-to-all-start.1) | async-done | bytes 69664 | tf_op jit(solution)/shard_map/all_to_all | solution.py:159
  62.9 0.6 broadcast_select_fusion
  (2 shorter events, 0.0 us)
Async XLA Ops:
  41.5 21.4 %all-to-all-start.1 = ((f32[256,1,68]{2,1,0:T(1,128)}), f32[256,1,68]{2,1,0:T(1,128)S(1)}, u32[]{:S(2)}, u32[]{:S(2)}) async-start(f32[256,1,68]{2,1,0:T(1,128)} %bitcast.12), calls=%async_computation.1 | async-start | bytes 262144 | tf_op jit(solution)/shard_map/all_to_all | solution.py:159

commit v4 on v3

--- a/solution.py
+++ b/solution.py
@@ -11,6 +11,14 @@
 LANES = 128
 VMEM = pl.BlockSpec(memory_space=pltpu.VMEM)
 ANY = pl.BlockSpec(memory_space=pl.ANY)
+
+
+def first_shard(shards):
+    return 3 * shards // 4 + 1
+
+
+def members(shards):
+    return [(first_shard(shards) - i) % shards for i in range(shards)]
 
 
 def join_kernel(offsets_hbm, a_ref, b_ref, out_ref, order_ref, offsets_ref, sems):
@@ -73,8 +81,9 @@
         (2 * (y_ref.shape[0] - tiles), LANES), y_ref.dtype)
 
     def split(s, carry):
-        flat(x_ref, 1 + s * per, per)[...] = flat(both_ref.at[s], 0, per)[...]
-        flat(y_ref, s * per, per)[...] = flat(both_ref.at[s], per, per)[...]
+        at = lax.rem(first_shard(shards) + shards - s, shards) * per
+        flat(x_ref, 1 + at, per)[...] = flat(both_ref.at[s], 0, per)[...]
+        flat(y_ref, at, per)[...] = flat(both_ref.at[s], per, per)[...]
         return carry
 
     lax.fori_loop(0, shards, split, 0, unroll=8)
@@ -115,8 +124,8 @@
     sums = jnp.sum(acc.reshape(blocks, 8, LANES), axis=1) * scale
     pieces, copies, width = out_ref.shape
     lane = lax.broadcasted_iota(jnp.int32, (copies, LANES), 1)
-    for q in range(pieces):
-        b, s = divmod(q * width, LANES)
+    for q, piece in enumerate(members(pieces)):
+        b, s = divmod(piece * width, LANES)
         row = jnp.broadcast_to(sums[b:b + 1], (copies, LANES))
         if s:
             row = pltpu.roll(row, LANES - s, 1)
@@ -150,14 +159,23 @@
     ctx_count, ch_count = lax.axis_size("ctx"), lax.axis_size("ch")
     scale = 1.0 / math.sqrt(tok_dev * ctx_count * local_ch * ch_count)
     both, order = joined(block_offsets, saved_input, out_grad)
-    both = lax.all_to_all(both, "ctx", split_axis=0, concat_axis=0, tiled=True)
+    both = lax.all_to_all(
+        both, "ctx", split_axis=0, concat_axis=0, tiled=True,
+        axis_index_groups=[members(ctx_count)])
     tiles = both.shape[2] // LANES
     both = both.reshape(ctx_count, local_ch, tiles, LANES).transpose(0, 2, 1, 3)
     blocks = block_offsets.shape[0] + 1
-    sums = lag_sums(both, order, blocks, scale, ctx_count, ch_count)
-    sums = sums.reshape(ctx_count * ch_count, -1)
-    got = lax.all_to_all(sums, ("ctx", "ch"), split_axis=0, concat_axis=0, tiled=True)
-    out = jnp.sum(got.reshape(filters, ch_count, -1), axis=1)
+    pairs = ch_count // 2
+    sums = lag_sums(both, order, blocks, scale, ctx_count, pairs)
+    groups = [
+        [c * ch_count + 2 * h + side for c in members(ctx_count) for h in (2, 3, 1, 0)]
+        for side in range(2)
+    ]
+    got = lax.all_to_all(
+        sums.reshape(ctx_count * pairs, -1), ("ctx", "ch"), split_axis=0, concat_axis=0, tiled=True,
+        axis_index_groups=groups)
+    out = jnp.sum(got.reshape(filters, pairs, -1), axis=1)
+    out = out + lax.ppermute(out, "ch", [(h, h ^ 1) for h in range(ch_count)])
     lag = lax.broadcasted_iota(jnp.int32, out.shape, 1) + lax.axis_index("ctx") * out.shape[1]
     return jnp.where((lag >= LANES) | (lag < head_len[0]), out, jnp.zeros_like(out))
 

time: 63.8 us -> 59.7 us (0.936)
  the two profiles are of different devices: /device:TPU:1 before, /device:TPU:6 now
where the time goes in v4:
time: 59.7 us; the launch traced here: 59.6 us
  blocking collectives  30.8 us (52%)
  starting transfers between devices  12.8 us (21%)
  waiting for transfers between devices  8.15 us (14%)
  Pallas kernels  6.38 us (11%)
  between operations  0.69 us (1%)
  other arithmetic  0.66 us (1%)
    all_to_all x1, blocking collectives, local(): lax.all_to_all(both, 'ctx', split_axis=0, concat_axis=0, tiled=True, axis...  30.8 us
    all_to_all x1, starting transfers between devices, local(): lax.all_to_all(sums.reshape(ctx_count * pairs, -1), ('ctx', 'ch'), split_...  12.7 us
    pallas_call x1, Pallas kernels, lag_sums(): pl.pallas_call(functools.partial(lag_kernel, scale), out_shape=jax.ShapeD...  5.24 us
    all_to_all x1, waiting for transfers between devices, local(): lax.all_to_all(sums.reshape(ctx_count * pairs, -1), ('ctx', 'ch'), split_...  4.44 us
    ppermute x1, waiting for transfers between devices, local(): out = out + lax.ppermute(out, 'ch', [(h, h ^ 1) for h in range(ch_count)])  3.71 us
  transfers between devices with their start and end apart: 2, of which 2 were waited for; matrix products, arithmetic and copies ran while one was open for 0% of the time, Pallas kernels for 0%

profile of v4, /device:TPU:6, one launch (start us, length us, event | category | flops | bytes accessed | tf_op | source)
XLA Modules:
  0.0 59.6 jit_solution(13108255070757416251)
XLA Ops:
  0.0 1.1 %shard_map.46 = (bf16[32,2,6144]{2,1,0:T(2,128)(2,1)S(1)}, s32[8,128]{1,0:T(8,128)S(1)}) custom-call(s32[16]{0:T(128)} %offsets_hbm.1, bf16[32,2,3072]{2,1,0:T(2,128)(2,1)} %a_ref.1, bf16[32,2,3072]{2,1,0:T(2,128)(2,1)} %b_ref.1), custom_call_target="tpu_custom_call" | custom-call | tf_op jit(solution)/shard_map/pallas_call | solution.py:53
  1.1 30.8 %all_to_all.14 = bf16[32,2,6144]{2,1,0:T(2,128)(2,1)S(1)} all-to-all(bf16[32,2,6144]{2,1,0:T(2,128)(2,1)S(1)} %get-tuple-element.8), channel_id=1, replica_groups={{200,192,184,176,168,160,152,144,136,128,120,112,104,96,88,80,72,64,56,..., dimensions={0} | all-to-all | bytes 1572864 | tf_op jit(solution)/shard_map/all_to_all | solution.py:162
  32.0 5.2 %shard_map.47 = f32[32,4,68]{2,1,0:T(4,128)} custom-call(s32[8,128]{1,0:T(8,128)S(1)} %get-tuple-element.7.order_vmem, bf16[32,48,2,128]{3,2,1,0:T(2,128)(2,1)S(1)} %bitcast.9), custom_call_target="tpu_custom_call" | custom-call | tf_op jit(solution)/shard_map/pallas_call | solution.py:141
  37.2 12.7 %all-to-all-start.1 = ((f32[128,1,68]{2,1,0:T(1,128)}), f32[128,1,68]{2,1,0:T(1,128)S(1)}, u32[]{:S(2)}, u32[]{:S(2)}) async-start(f32[128,1,68]{2,1,0:T(1,128)} %bitcast.11), calls=%async_computation.1 | async-start | bytes 131072 | tf_op jit(solution)/shard_map/all_to_all | solution.py:174
  50.6 4.4 %all-to-all-done.1 = f32[128,1,68]{2,1,0:T(1,128)S(1)} async-done(((f32[128,1,68]{2,1,0:T(1,128)}), f32[128,1,68]{2,1,0:T(1,128)S(1)}, u32[]{:S(2)}, u32[]{:S(2)}) %all-to-all-start.1) | async-done | bytes 34848 | tf_op jit(solution)/shard_map/all_to_all | solution.py:174
  55.1 0.1 collective-permute-start
  55.2 3.7 %collective-permute-done = f32[32,68]{1,0:T(8,128)S(1)} collective-permute-done((f32[32,68]{1,0:T(8,128)S(1)}, f32[32,68]{1,0:T(8,128)S(1)}, u32[]{:S(2)}, u32[]{:S(2)}) %collective-permute-start) | collective-permute-done | bytes 8736 | tf_op jit(solution)/shard_map/ppermute | solution.py:178
  59.0 0.6 %add_select_fusion = f32[32,68]{1,0:T(8,128)} fusion(f32[32,68]{1,0:T(8,128)S(1)} %reduce_sum.9, f32[32,68]{1,0:T(8,128)S(1)} %collective-permute-done, pred[68]{0:T(512)(128)(4,1)S(1)} %compare_or_fusion), kind=kLoop, calls=%fused_computation | loop fusion | flops 4352 | bytes 26180 | tf_op jit(solution)/shard_map/jit(_where)/select_n | solution.py:180
  (2 shorter events, 0.1 us)
Async XLA Ops:
  37.2 17.8 %all-to-all-start.1 = ((f32[128,1,68]{2,1,0:T(1,128)}), f32[128,1,68]{2,1,0:T(1,128)S(1)}, u32[]{:S(2)}, u32[]{:S(2)}) async-start(f32[128,1,68]{2,1,0:T(1,128)} %bitcast.11), calls=%async_computation.1 | async-start | bytes 131072 | tf_op jit(solution)/shard_map/all_to_all | solution.py:174
  55.1 3.8 %collective-permute-start = (f32[32,68]{1,0:T(8,128)S(1)}, f32[32,68]{1,0:T(8,128)S(1)}, u32[]{:S(2)}, u32[]{:S(2)}) collective-permute-start(f32[32,68]{1,0:T(8,128)S(1)} %reduce_sum.9), channel_id=1, source_target_pairs={{0,1},{1,0},{2,3},{3,2},{4,5},{5,4},{6,7},{7,6},{8,9},{9,8},{10,11... | collective-permute-start | bytes 26120 | tf_op jit(solution)/shard_map/ppermute | solution.py:178

commit v5 on v4

--- a/solution.py
+++ b/solution.py
@@ -140,7 +140,7 @@
     tiles = shards * pair_tiles // 2
     return pl.pallas_call(
         functools.partial(lag_kernel, scale),
-        out_shape=jax.ShapeDtypeStruct((pieces, copies, blocks * LANES // pieces), jnp.float32),
+        out_shape=pltpu.VMEM((pieces, copies, blocks * LANES // pieces), jnp.float32),
         in_specs=[VMEM, VMEM],
         out_specs=VMEM,
         scratch_shapes=[
@@ -152,6 +152,21 @@
             pltpu.SemaphoreType.DMA,
         ],
     )(*(pltpu.with_memory_space_constraint(a, pltpu.VMEM) for a in (order, both)))
+
+
+def finish_kernel(head_ref, a_ref, b_ref, out_ref):
+    total = a_ref[...] + b_ref[...]
+    lag = lax.broadcasted_iota(jnp.int32, total.shape, 1) + lax.axis_index("ctx") * total.shape[1]
+    out_ref[...] = jnp.where((lag >= LANES) | (lag < head_ref[0]), total, jnp.zeros_like(total))
+
+
+def finished(head_len, a, b):
+    return pl.pallas_call(
+        finish_kernel,
+        out_shape=jax.ShapeDtypeStruct(a.shape, a.dtype),
+        in_specs=[pl.BlockSpec(memory_space=pltpu.SMEM), VMEM, VMEM],
+        out_specs=VMEM,
+    )(head_len, *(pltpu.with_memory_space_constraint(p, pltpu.VMEM) for p in (a, b)))
 
 
 def local(saved_input, out_grad, block_offsets, head_len):
@@ -175,9 +190,9 @@
         sums.reshape(ctx_count * pairs, -1), ("ctx", "ch"), split_axis=0, concat_axis=0, tiled=True,
         axis_index_groups=groups)
     out = jnp.sum(got.reshape(filters, pairs, -1), axis=1)
-    out = out + lax.ppermute(out, "ch", [(h, h ^ 1) for h in range(ch_count)])
-    lag = lax.broadcasted_iota(jnp.int32, out.shape, 1) + lax.axis_index("ctx") * out.shape[1]
-    return jnp.where((lag >= LANES) | (lag < head_len[0]), out, jnp.zeros_like(out))
+    out, head_len = lax.optimization_barrier((out, head_len))
+    twin = lax.ppermute(out, "ch", [(h, h ^ 1) for h in range(ch_count)])
+    return finished(head_len, out, twin)
 
 
 def solution(mesh):

time: 59.7 us -> 58.9 us (0.987)
  blocking collectives: 30.8 us -> 48.5 us
  starting transfers between devices: 12.8 us -> 0.09 us
  waiting for transfers between devices: 8.15 us -> 3.08 us
  other arithmetic: 0.66 us -> 0.04 us
    all_to_all x0 -> x1, blocking collectives: none -> 17.6 us  [local(): lax.all_to_all(sums.reshape(ctx_count * pairs, -1), ('ctx', 'ch'), split_...]
    all_to_all x1 -> x0, starting transfers between devices: 12.7 us -> none  [local(): lax.all_to_all(sums.reshape(ctx_count * pairs, -1), ('ctx', 'ch'), split_...]
    all_to_all x1 -> x0, waiting for transfers between devices: 4.44 us -> none  [local(): lax.all_to_all(sums.reshape(ctx_count * pairs, -1), ('ctx', 'ch'), split_...]
    ppermute x1, waiting for transfers between devices: 3.71 us -> 3.08 us  [local(): twin = lax.ppermute(out, 'ch', [(h, h ^ 1) for h in range(ch_count)])]
    select_n x1 -> x0, other arithmetic: 0.61 us -> none  [local(): jnp.where((lag >= LANES) | (lag < head_len[0]), out, jnp.zeros_like(out))]
    pallas_call x1 -> x2, Pallas kernels: 5.24 us -> 5.23 us  [the longest x1 4.62 us: lag_sums(): pl.pallas_call(functools.partial(lag_kernel, scale), out_shape=pltpu.VMEM...]
  transfers between devices with their start and end apart: 2 -> 1, of which waited for: 2 -> 1; matrix products, arithmetic and copies ran while one was open for 0% -> 0% of each run, Pallas kernels for 0% -> 0%
where the time goes in v5:
time: 58.9 us; the launch traced here: 58.7 us
  blocking collectives  48.5 us (82%)
  Pallas kernels  6.37 us (11%)
  waiting for transfers between devices  3.08 us (5%)
  between operations  0.68 us (1%)
    all_to_all x1, blocking collectives, local(): lax.all_to_all(both, 'ctx', split_axis=0, concat_axis=0, tiled=True, axis...  30.8 us
    all_to_all x1, blocking collectives, local(): lax.all_to_all(sums.reshape(ctx_count * pairs, -1), ('ctx', 'ch'), split_...  17.6 us
    pallas_call x1, Pallas kernels, lag_sums(): pl.pallas_call(functools.partial(lag_kernel, scale), out_shape=pltpu.VMEM...  4.62 us
    ppermute x1, waiting for transfers between devices, local(): twin = lax.ppermute(out, 'ch', [(h, h ^ 1) for h in range(ch_count)])  3.08 us
  transfers between devices with their start and end apart: 1, of which 1 were waited for; matrix products, arithmetic and copies ran while one was open for 0% of the time, Pallas kernels for 0%

profile of v5, /device:TPU:6, one launch (start us, length us, event | category | flops | bytes accessed | tf_op | source)
XLA Modules:
  0.0 58.7 jit_solution(13535768351885191255)
XLA Ops:
  0.0 1.1 %shard_map.46 = (bf16[32,2,6144]{2,1,0:T(2,128)(2,1)S(1)}, s32[8,128]{1,0:T(8,128)S(1)}) custom-call(s32[16]{0:T(128)} %offsets_hbm.1, bf16[32,2,3072]{2,1,0:T(2,128)(2,1)} %a_ref.1, bf16[32,2,3072]{2,1,0:T(2,128)(2,1)} %b_ref.1), custom_call_target="tpu_custom_call" | custom-call | tf_op jit(solution)/shard_map/pallas_call | solution.py:53
  1.1 30.8 %all_to_all.14 = bf16[32,2,6144]{2,1,0:T(2,128)(2,1)S(1)} all-to-all(bf16[32,2,6144]{2,1,0:T(2,128)(2,1)S(1)} %get-tuple-element.10), channel_id=1, replica_groups={{200,192,184,176,168,160,152,144,136,128,120,112,104,96,88,80,72,64,56,..., dimensions={0} | all-to-all | bytes 1572864 | tf_op jit(solution)/shard_map/all_to_all | solution.py:177
  32.0 4.6 %shard_map.47 = f32[32,4,68]{2,1,0:T(4,128)S(1)} custom-call(s32[8,128]{1,0:T(8,128)S(1)} %get-tuple-element.9.order_vmem, bf16[32,48,2,128]{3,2,1,0:T(2,128)(2,1)S(1)} %bitcast.7), custom_call_target="tpu_custom_call" | custom-call | tf_op jit(solution)/shard_map/pallas_call | solution.py:141
  36.6 17.6 %all_to_all.15 = f32[128,1,68]{2,1,0:T(1,128)S(1)} all-to-all(f32[128,1,68]{2,1,0:T(1,128)S(1)} %bitcast.8), channel_id=1, replica_groups={{204,206,202,200,196,198,194,192,188,190,186,184,180,182,178,176,172,17..., dimensions={0} | all-to-all | bytes 69632 | tf_op jit(solution)/shard_map/all_to_all | solution.py:189
  54.3 0.1 collective-permute-start
  55.0 3.1 %collective-permute-done.b_ref = f32[32,68]{1,0:T(8,128)S(1)} collective-permute-done((f32[32,68]{1,0:T(8,128)S(1)}, f32[32,68]{1,0:T(8,128)S(1)}, u32[]{:S(2)}, u32[]{:S(2)}) %collective-permute-start) | collective-permute-done | bytes 8736 | tf_op jit(solution)/shard_map/ppermute | solution.py:194
  58.1 0.6 %shard_map.48 = f32[32,68]{1,0:T(8,128)} custom-call(s32[1]{0:T(128)S(6)} %copy.6.head_ref, f32[32,68]{1,0:T(8,128)S(1)} %reduce_sum.9.a_ref, f32[32,68]{1,0:T(8,128)S(1)} %collective-permute-done.b_ref), custom_call_target="tpu_custom_call" | custom-call | tf_op jit(solution)/shard_map/pallas_call | solution.py:164
  (1 shorter events, 0.0 us)
Async XLA Ops:
  54.3 3.8 %collective-permute-start = (f32[32,68]{1,0:T(8,128)S(1)}, f32[32,68]{1,0:T(8,128)S(1)}, u32[]{:S(2)}, u32[]{:S(2)}) collective-permute-start(f32[32,68]{1,0:T(8,128)S(1)} %reduce_sum.9.a_ref), channel_id=1, source_target_pairs={{0,1},{1,0},{2,3},{3,2},{4,5},{5,4},{6,7},{7,6},{8,9},{9,8},{10,11... | collective-permute-start | bytes 26120 | tf_op jit(solution)/shard_map/ppermute | solution.py:194

commit v6 on v5

--- a/solution.py
+++ b/solution.py
@@ -182,16 +182,14 @@
     blocks = block_offsets.shape[0] + 1
     pairs = ch_count // 2
     sums = lag_sums(both, order, blocks, scale, ctx_count, pairs)
-    groups = [
-        [c * ch_count + 2 * h + side for c in members(ctx_count) for h in (2, 3, 1, 0)]
-        for side in range(2)
-    ]
+    halves = [(h + pairs // 2) % pairs for h in range(pairs)], range(pairs, ch_count)
+    groups = [[c * ch_count + h for c in members(ctx_count) for h in half] for half in halves]
     got = lax.all_to_all(
         sums.reshape(ctx_count * pairs, -1), ("ctx", "ch"), split_axis=0, concat_axis=0, tiled=True,
         axis_index_groups=groups)
     out = jnp.sum(got.reshape(filters, pairs, -1), axis=1)
     out, head_len = lax.optimization_barrier((out, head_len))
-    twin = lax.ppermute(out, "ch", [(h, h ^ 1) for h in range(ch_count)])
+    twin = lax.ppermute(out, "ch", [(h, (ch_count - 1 - h) ^ 1) for h in range(ch_count)])
     return finished(head_len, out, twin)
 
 

time: 58.9 us -> 58.2 us (0.988)
  the two profiles are of different devices: /device:TPU:6 before, /device:TPU:1 now
where the time goes in v6:
time: 58.2 us; the launch traced here: 57.4 us
  blocking collectives  47.7 us (82%)
  Pallas kernels  5.76 us (10%)
  starting transfers between devices  2.7 us (5%)
  between operations  0.67 us (1%)
    all_to_all x1, blocking collectives, local(): lax.all_to_all(both, 'ctx', split_axis=0, concat_axis=0, tiled=True, axis...  31.8 us
    all_to_all x1, blocking collectives, local(): lax.all_to_all(sums.reshape(ctx_count * pairs, -1), ('ctx', 'ch'), split_...  15.9 us
    pallas_call x1, Pallas kernels, lag_sums(): pl.pallas_call(functools.partial(lag_kernel, scale), out_shape=pltpu.VMEM...  4.01 us
    ppermute x1, starting transfers between devices, local(): lax.ppermute(out, 'ch', [(h, ch_count - 1 - h ^ 1) for h in range(ch_coun...  2.7 us
  transfers between devices with their start and end apart: 1, of which 1 were waited for; matrix products, arithmetic and copies ran while one was open for 0% of the time, Pallas kernels for 0%

profile of v6, /device:TPU:1, one launch (start us, length us, event | category | flops | bytes accessed | tf_op | source)
XLA Modules:
  0.0 57.4 jit_solution(12820309367013557924)
XLA Ops:
  0.0 1.1 %shard_map.46 = (bf16[32,2,6144]{2,1,0:T(2,128)(2,1)S(1)}, s32[8,128]{1,0:T(8,128)S(1)}) custom-call(s32[16]{0:T(128)} %offsets_hbm.1, bf16[32,2,3072]{2,1,0:T(2,128)(2,1)} %a_ref.1, bf16[32,2,3072]{2,1,0:T(2,128)(2,1)} %b_ref.1), custom_call_target="tpu_custom_call" | custom-call | tf_op jit(solution)/shard_map/pallas_call | solution.py:53
  1.1 31.8 %all_to_all.14 = bf16[32,2,6144]{2,1,0:T(2,128)(2,1)S(1)} all-to-all(bf16[32,2,6144]{2,1,0:T(2,128)(2,1)S(1)} %get-tuple-element.10), channel_id=1, replica_groups={{200,192,184,176,168,160,152,144,136,128,120,112,104,96,88,80,72,64,56,..., dimensions={0} | all-to-all | bytes 1572864 | tf_op jit(solution)/shard_map/all_to_all | solution.py:177
  33.0 4.0 %shard_map.47 = f32[32,4,68]{2,1,0:T(4,128)S(1)} custom-call(s32[8,128]{1,0:T(8,128)S(1)} %get-tuple-element.9.order_vmem, bf16[32,48,2,128]{3,2,1,0:T(2,128)(2,1)S(1)} %bitcast.7), custom_call_target="tpu_custom_call" | custom-call | tf_op jit(solution)/shard_map/pallas_call | solution.py:141
  37.0 15.9 %all_to_all.15 = f32[128,1,68]{2,1,0:T(1,128)S(1)} all-to-all(f32[128,1,68]{2,1,0:T(1,128)S(1)} %bitcast.8), channel_id=1, replica_groups={{202,203,200,201,194,195,192,193,186,187,184,185,178,179,176,177,170,17..., dimensions={0} | all-to-all | bytes 69632 | tf_op jit(solution)/shard_map/all_to_all | solution.py:187
  52.9 2.7 %collective-permute-start = (f32[32,68]{1,0:T(8,128)S(1)}, f32[32,68]{1,0:T(8,128)S(1)}, u32[]{:S(2)}, u32[]{:S(2)}) collective-permute-start(f32[32,68]{1,0:T(8,128)S(1)} %reduce_sum.9.a_ref), channel_id=1, source_target_pairs={{0,6},{1,7},{2,4},{3,5},{4,2},{5,3},{6,0},{7,1},{8,14},{9,15},{10,... | collective-permute-start | bytes 26120 | tf_op jit(solution)/shard_map/ppermute | solution.py:192
  56.3 0.5 collective-permute-done.b_ref
  56.8 0.6 %shard_map.48 = f32[32,68]{1,0:T(8,128)} custom-call(s32[1]{0:T(128)S(6)} %copy.6.head_ref, f32[32,68]{1,0:T(8,128)S(1)} %reduce_sum.9.a_ref, f32[32,68]{1,0:T(8,128)S(1)} %collective-permute-done.b_ref), custom_call_target="tpu_custom_call" | custom-call | tf_op jit(solution)/shard_map/pallas_call | solution.py:164
  (1 shorter events, 0.0 us)
Async XLA Ops:
  52.9 3.9 %collective-permute-start = (f32[32,68]{1,0:T(8,128)S(1)}, f32[32,68]{1,0:T(8,128)S(1)}, u32[]{:S(2)}, u32[]{:S(2)}) collective-permute-start(f32[32,68]{1,0:T(8,128)S(1)} %reduce_sum.9.a_ref), channel_id=1, source_target_pairs={{0,6},{1,7},{2,4},{3,5},{4,2},{5,3},{6,0},{7,1},{8,14},{9,15},{10,... | collective-permute-start | bytes 26120 | tf_op jit(solution)/shard_map/ppermute | solution.py:192

commit v7 on v6

--- a/solution.py
+++ b/solution.py
@@ -14,7 +14,7 @@
 
 
 def first_shard(shards):
-    return 3 * shards // 4 + 1
+    return 3 * shards // 4 + 3
 
 
 def members(shards):

time: 58.2 us -> 58.2 us (level)
  no operation moved by 1% of the time
where the time goes in v7:
time: 58.2 us; the launch traced here: 57.7 us
  blocking collectives  47.7 us (82%)
  Pallas kernels  6.06 us (10%)
  starting transfers between devices  2.7 us (5%)
  between operations  0.67 us (1%)
    all_to_all x1, blocking collectives, local(): lax.all_to_all(both, 'ctx', split_axis=0, concat_axis=0, tiled=True, axis...  31.8 us
    all_to_all x1, blocking collectives, local(): lax.all_to_all(sums.reshape(ctx_count * pairs, -1), ('ctx', 'ch'), split_...  15.9 us
    pallas_call x1, Pallas kernels, lag_sums(): pl.pallas_call(functools.partial(lag_kernel, scale), out_shape=pltpu.VMEM...  4.31 us
    ppermute x1, starting transfers between devices, local(): lax.ppermute(out, 'ch', [(h, ch_count - 1 - h ^ 1) for h in range(ch_coun...  2.7 us
  transfers between devices with their start and end apart: 1, of which 1 were waited for; matrix products, arithmetic and copies ran while one was open for 0% of the time, Pallas kernels for 0%

profile of v7, /device:TPU:1, one launch (start us, length us, event | category | flops | bytes accessed | tf_op | source)
XLA Modules:
  0.0 57.7 jit_solution(13677979608000832614)
XLA Ops:
  0.0 1.1 %shard_map.46 = (bf16[32,2,6144]{2,1,0:T(2,128)(2,1)S(1)}, s32[8,128]{1,0:T(8,128)S(1)}) custom-call(s32[16]{0:T(128)} %offsets_hbm.1, bf16[32,2,3072]{2,1,0:T(2,128)(2,1)} %a_ref.1, bf16[32,2,3072]{2,1,0:T(2,128)(2,1)} %b_ref.1), custom_call_target="tpu_custom_call" | custom-call | tf_op jit(solution)/shard_map/pallas_call | solution.py:53
  1.1 31.8 %all_to_all.14 = bf16[32,2,6144]{2,1,0:T(2,128)(2,1)S(1)} all-to-all(bf16[32,2,6144]{2,1,0:T(2,128)(2,1)S(1)} %get-tuple-element.10), channel_id=1, replica_groups={{216,208,200,192,184,176,168,160,152,144,136,128,120,112,104,96,88,80,7..., dimensions={0} | all-to-all | bytes 1572864 | tf_op jit(solution)/shard_map/all_to_all | solution.py:177
  32.9 4.3 %shard_map.47 = f32[32,4,68]{2,1,0:T(4,128)S(1)} custom-call(s32[8,128]{1,0:T(8,128)S(1)} %get-tuple-element.9.order_vmem, bf16[32,48,2,128]{3,2,1,0:T(2,128)(2,1)S(1)} %bitcast.7), custom_call_target="tpu_custom_call" | custom-call | tf_op jit(solution)/shard_map/pallas_call | solution.py:141
  37.2 15.9 %all_to_all.15 = f32[128,1,68]{2,1,0:T(1,128)S(1)} all-to-all(f32[128,1,68]{2,1,0:T(1,128)S(1)} %bitcast.8), channel_id=1, replica_groups={{218,219,216,217,210,211,208,209,202,203,200,201,194,195,192,193,186,18..., dimensions={0} | all-to-all | bytes 69632 | tf_op jit(solution)/shard_map/all_to_all | solution.py:187
  53.2 2.7 %collective-permute-start = (f32[32,68]{1,0:T(8,128)S(1)}, f32[32,68]{1,0:T(8,128)S(1)}, u32[]{:S(2)}, u32[]{:S(2)}) collective-permute-start(f32[32,68]{1,0:T(8,128)S(1)} %reduce_sum.9.a_ref), channel_id=1, source_target_pairs={{0,6},{1,7},{2,4},{3,5},{4,2},{5,3},{6,0},{7,1},{8,14},{9,15},{10,... | collective-permute-start | bytes 26120 | tf_op jit(solution)/shard_map/ppermute | solution.py:192
  56.5 0.5 collective-permute-done.b_ref
  57.1 0.6 %shard_map.48 = f32[32,68]{1,0:T(8,128)} custom-call(s32[1]{0:T(128)S(6)} %copy.6.head_ref, f32[32,68]{1,0:T(8,128)S(1)} %reduce_sum.9.a_ref, f32[32,68]{1,0:T(8,128)S(1)} %collective-permute-done.b_ref), custom_call_target="tpu_custom_call" | custom-call | tf_op jit(solution)/shard_map/pallas_call | solution.py:164
  (1 shorter events, 0.0 us)
Async XLA Ops:
  53.2 3.9 %collective-permute-start = (f32[32,68]{1,0:T(8,128)S(1)}, f32[32,68]{1,0:T(8,128)S(1)}, u32[]{:S(2)}, u32[]{:S(2)}) collective-permute-start(f32[32,68]{1,0:T(8,128)S(1)} %reduce_sum.9.a_ref), channel_id=1, source_target_pairs={{0,6},{1,7},{2,4},{3,5},{4,2},{5,3},{6,0},{7,1},{8,14},{9,15},{10,... | collective-permute-start | bytes 26120 | tf_op jit(solution)/shard_map/ppermute | solution.py:192
